TPU v7x, 32 devices: a whole 2x2x4 slice. The times are simulated.
32 devices in a mesh: node: 4 (over y, x), wide: 8 (over z, core).
Axes of the slice: x: 2, y: 2, z: 4, core: 2. Of those that a mesh axis runs over, the one named last changes fastest.
Arguments:
- feats: bfloat16 [8192, 40], P(('node', 'wide')), may hold values from -6 to 6
- utt_lengths: int32 [32, 8], P(('node', 'wide')), may hold values from 1 to 128, 256 in all within a row
- frame_mask: int32 [8192], P(('node', 'wide')), may hold values from 0 to 1, as said below
- targets: int32 [8192], P(('node', 'wide')), may hold values from 0 to 9303
- val_feats: bfloat16 [4096, 40], P(('node', 'wide')), may hold values from -6 to 6
- val_mask: int32 [4096], P(('node', 'wide')), may hold values from 0 to 1, as said below
- val_targets: int32 [4096], P(('node', 'wide')), may hold values from 0 to 9303
- master: float32 [47200, 512], P(('node', 'wide')), as said below
- first_moment: float32 [47200, 512], P(('node', 'wide')), may hold values from -0.0012207031 to 0.0012207031
- second_moment: float32 [47200, 512], P(('node', 'wide')), may hold values from 8.275953e-09 to 8.2759534e-08
- residual: float32 [377600, 512], P(('node', 'wide')), as said below
- average: float32 [47200, 512], P(('node', 'wide')), as said below
Outputs:
- loss: float32 [], replicated
- val_loss: float32 [], replicated
- grad_norm: float32 [], replicated
- master_new: float32 [47200, 512], P(('node', 'wide'))
- first_new: float32 [47200, 512], P(('node', 'wide'))
- second_new: float32 [47200, 512], P(('node', 'wide'))
- residual_new: float32 [377600, 512], P(('node', 'wide'))
- average_new: float32 [47200, 512], P(('node', 'wide'))
Inputs may be any that keep to these rules, and one draw needn't show every extreme that they name: `frame_mask`: the first frame of every device counts; the share of counted frames rises over the devices in order from about a quarter to all. `val_mask`: the first validation frame of every device counts; the share of counted frames rises over the devices in order from about a quarter to all. `utt_lengths`: each row fills the device's 256 frames. `master`: parameters of order of their layer's usual scale. `average`: like master. `residual`: real values of either sign.
All inputs are finite; a program needn't handle non-finite values.
Results may differ from a plain program's by a relative error of at most 0.0003.
The roundings to bfloat16 on the way count: a program that leaves them out, or rounds other values in their place, can miss the bound.
Values may be sent and summed in bfloat16 or wider, within the bound.
No kernel may reach another device: no remote copies, remote signals or barrier semaphores. Data moves between devices by JAX's collectives and lax.ppermute only.
A program may use at most 640 MiB of HBM per device.

v0:
```python
import math

import jax
import jax.numpy as jnp
from jax import lax
from jax.sharding import PartitionSpec as P

CONTEXT = 11
UNITS = 2048
SENONES = 9304
D_IN = 440
STEP_COUNT = 8
PARAMS = 24163416


CLIP_NORM = 1.0
LEARN_RATE = 0.02
BETA_ONE = 0.5
BETA_TWO = 0.5
DECAY = 0.1
AVG_KEEP = 0.9
EPS_ADAM = 1e-08


def stack_frames(feats, lengths):
    count = feats.shape[0]
    ends = jnp.cumsum(lengths)
    starts = ends - lengths
    where_t = jnp.arange(count, dtype=jnp.int32)[:, None]
    inside = (where_t >= starts[None, :]) & (where_t < ends[None, :])
    first = jnp.sum(jnp.where(inside, starts[None, :], 0), axis=1)
    last = jnp.sum(jnp.where(inside, ends[None, :], 0), axis=1) - 1
    offsets = jnp.arange(CONTEXT, dtype=jnp.int32) - CONTEXT // 2
    index = jnp.clip(where_t + offsets[None, :], first[:, None], last[:, None])
    return feats[index].reshape(count, CONTEXT * feats.shape[1])


def unpack(flat):
    line = flat.reshape(-1)
    shapes = [(D_IN, UNITS), (UNITS,), (UNITS, UNITS), (UNITS,), (UNITS, SENONES), (SENONES,)]
    pieces = []
    start = 0
    for shape in shapes:
        length = math.prod(shape)
        pieces.append(line[start : start + length].reshape(shape))
        start = start + length
    return tuple(pieces)


def layer_forward(inputs, weight, bias):
    return jnp.dot(inputs, weight, preferred_element_type=jnp.float32) + bias.astype(jnp.float32)


def layer_backward(inputs, weight, delta, need_input):
    grad_weight = lax.dot_general(
        inputs, delta, (((0,), (0,)), ((), ())), preferred_element_type=jnp.float32
    )
    grad_bias = jnp.sum(delta.astype(jnp.float32), axis=0)
    grad_input = None
    if need_input:
        grad_input = lax.dot_general(
            delta, weight, (((1,), (1,)), ((), ())), preferred_element_type=jnp.float32
        )
    return (grad_weight, grad_bias, grad_input)


def run_layers(params, stacked):
    w_in, b_in, w_mid, b_mid, w_out, b_out = params
    sig_one = jax.nn.sigmoid(layer_forward(stacked, w_in, b_in))
    h_one = sig_one.astype(jnp.bfloat16)
    sig_two = jax.nn.sigmoid(layer_forward(h_one, w_mid, b_mid))
    h_two = sig_two.astype(jnp.bfloat16)
    logits = layer_forward(h_two, w_out, b_out)
    return (sig_one, h_one, sig_two, h_two, logits)


def frame_terms(logits, labels, weights):
    lse = jax.nn.logsumexp(logits, axis=1)
    picked = jnp.take_along_axis(logits, labels[:, None], axis=1)[:, 0]
    return (jnp.sum(weights * (lse - picked)), lse)


def pack_signs(rest):
    bits = (rest >= 0).astype(jnp.int32).reshape(rest.shape[0], rest.shape[1] // 32, 32)
    shifts = jnp.arange(32, dtype=jnp.int32)
    return jnp.sum(jnp.left_shift(bits, shifts), axis=2)


def unpack_signs(words):
    shifts = jnp.arange(32, dtype=jnp.int32)
    bits = jnp.bitwise_and(jnp.right_shift(words[..., None], shifts), 1)
    signs = (2 * bits - 1).astype(jnp.float32)
    return signs.reshape(words.shape[:-1] + (words.shape[-1] * 32,))


def body(
    feats,
    utt_lengths,
    frame_mask,
    targets,
    val_feats,
    val_mask,
    val_targets,
    master,
    first_moment,
    second_moment,
    residual,
    average,
):
    width = master.shape[1]
    shard_rows = master.shape[0]
    quarter_rows = residual.shape[0]
    wide_count = lax.axis_size("wide")
    gathered = lax.all_gather(master.astype(jnp.bfloat16), ("node", "wide"), axis=0, tiled=True)
    total_rows = gathered.shape[0]
    params = unpack(gathered)
    w_in, b_in, w_mid, b_mid, w_out, b_out = params
    stacked = stack_frames(feats, utt_lengths[0])
    weights = frame_mask.astype(jnp.float32)
    sig_one, h_one, sig_two, h_two, logits = run_layers(params, stacked)
    loss_part, lse = frame_terms(logits, targets, weights)
    count_part = jnp.sum(weights)
    loss_sum, count = lax.psum((loss_part, count_part), ("node", "wide"))
    probs = jnp.exp(logits - lse[:, None])
    hit = targets[:, None] == lax.broadcasted_iota(jnp.int32, logits.shape, 1)
    delta_out = (weights[:, None] * jnp.where(hit, probs - 1.0, probs)).astype(jnp.bfloat16)
    g_out, gb_out, back_two = layer_backward(h_two, w_out, delta_out, True)
    filler = jnp.zeros((total_rows * width - PARAMS,), jnp.float32)
    delta_two = (back_two * (sig_two * (1.0 - sig_two))).astype(jnp.bfloat16)
    g_mid, gb_mid, back_one = layer_backward(h_one, w_mid, delta_two, True)
    delta_one = (back_one * (sig_one * (1.0 - sig_one))).astype(jnp.bfloat16)
    g_in, gb_in, unused = layer_backward(stacked, w_in, delta_one, False)
    pieces = [g_in, gb_in, g_mid, gb_mid, g_out, gb_out]
    grad_flat = jnp.concatenate([piece.reshape(-1) for piece in pieces] + [filler]).reshape(
        total_rows, width
    )
    quarter = lax.psum_scatter(grad_flat, "node", scatter_dimension=0, tiled=True)
    values = quarter + residual
    signs = jnp.where(residual >= 0, 1.0, -1.0).astype(jnp.float32)
    blocks = (signs * values).reshape(wide_count, shard_rows, width)
    scales = jnp.mean(blocks, axis=1)
    coded = (signs.reshape(wide_count, shard_rows, width) * scales[:, None, :]).reshape(
        quarter_rows, width
    )
    residual_new = values - coded
    words = pack_signs(residual)
    wide_at = lax.axis_index("wide")
    all_words = lax.all_gather(words, "wide", axis=0, tiled=True).reshape(
        wide_count, quarter_rows, width // 32
    )
    own_words = lax.dynamic_slice_in_dim(all_words, wide_at * shard_rows, shard_rows, 1)
    all_scales = lax.all_gather(scales, "wide", axis=0, tiled=True).reshape(
        wide_count, wide_count, width
    )
    own_scales = lax.dynamic_index_in_dim(all_scales, wide_at, 1, keepdims=False)
    decoded = jnp.sum(unpack_signs(own_words) * own_scales[:, None, :], axis=0)
    square_part = jnp.sum(decoded * decoded)
    square_sum = lax.psum(square_part, ("node", "wide"))
    grad_norm = jnp.sqrt(square_sum) / count
    factor = jnp.minimum(1.0, CLIP_NORM / (grad_norm + 1e-06))
    grad = decoded * (factor / count)
    first_new = BETA_ONE * first_moment + (1.0 - BETA_ONE) * grad
    second_new = BETA_TWO * second_moment + (1.0 - BETA_TWO) * grad * grad
    first_hat = first_new / (1.0 - BETA_ONE**STEP_COUNT)
    second_hat = second_new / (1.0 - BETA_TWO**STEP_COUNT)
    master_new = master - LEARN_RATE * (
        first_hat / (jnp.sqrt(second_hat) + EPS_ADAM) + DECAY * master
    )
    average_new = AVG_KEEP * average + (1.0 - AVG_KEEP) * master_new
    full_average = lax.all_gather(
        average_new.astype(jnp.bfloat16), ("node", "wide"), axis=0, tiled=True
    )
    val_params = unpack(full_average)
    val_stacked = stack_frames(val_feats, jnp.full((1,), val_feats.shape[0], jnp.int32))
    val_logits = run_layers(val_params, val_stacked)[4]
    val_weights = val_mask.astype(jnp.float32)
    val_part, val_lse = frame_terms(val_logits, val_targets, val_weights)
    val_sum, val_count = lax.psum((val_part, jnp.sum(val_weights)), ("node", "wide"))
    return (
        loss_sum / count,
        val_sum / val_count,
        grad_norm,
        master_new,
        first_new,
        second_new,
        residual_new,
        average_new,
    )


def solution(mesh):
    return jax.shard_map(
        body,
        mesh=mesh,
        in_specs=(
            P(("node", "wide"), None),
            P(("node", "wide"), None),
            P(("node", "wide")),
            P(("node", "wide")),
            P(("node", "wide"), None),
            P(("node", "wide")),
            P(("node", "wide")),
            P(("node", "wide"), None),
            P(("node", "wide"), None),
            P(("node", "wide"), None),
            P(("node", "wide"), None),
            P(("node", "wide"), None),
        ),
        out_specs=(
            P(),
            P(),
            P(),
            P(("node", "wide"), None),
            P(("node", "wide"), None),
            P(("node", "wide"), None),
            P(("node", "wide"), None),
            P(("node", "wide"), None),
        ),
        check_vma=False,
    )
```

profile of v0, /device:TPU:0, one launch (start us, length us, event | category | flops | bytes accessed | tf_op | source)
XLA Modules:
  0.0 4068.7 jit_solution(2934177250547230535)
XLA Ops:
  7.2 3.2 convert_bitcast_fusion.1
  10.5 24.8 copy.85
  35.2 11.6 shift-left_reduce_fusion
  47.8 5.6 gather_fusion
  53.9 226.1 %all-gather.7.cloned.1.call-done = bf16[32,1475,512]{2,1,0:T(8,128)(2,1)} async-done(((bf16[1,1475,512]{2,1,0:T(8,128)(2,1)}), bf16[32,1475,512]{2,1,0:T(8,128)(2,1)}) %all-gather.7.cloned.1.call-update) | async-done | bytes 48332816 | tf_op jit(solution)/shard_map/all_gather | solution.py:114
  280.0 50.0 %reshape.466 = bf16[47200,512]{1,0:T(8,128)(2,1)} reshape(bf16[32,1475,512]{2,1,0:T(8,128)(2,1)} %all-gather.7.cloned.1.call-done) | data formatting | bytes 96665600
  330.7 8.9 slice.68
  339.6 25.1 slice.70
  364.7 2.3 reshape.401
  367.0 14.0 reshape.402
  380.9 116.2 %reshape.403 = bf16[2048,9304]{1,0:T(8,128)(2,1)} reshape(bf16[37216,512]{1,0:T(8,128)(2,1)} %slice.70) | data formatting | bytes 76218368 | tf_op jit(solution)/shard_map/reshape | solution.py:45
  497.1 43.2 %reshape.404 = bf16[24166400]{0:T(1024)(128)(2,1)} reshape(bf16[32,1475,512]{2,1,0:T(8,128)(2,1)} %all-gather.7.cloned.1.call-done) | data formatting | bytes 96665600 | tf_op jit(solution)/shard_map/reshape | solution.py:39
  541.1 2.5 fusion.13
  545.7 2.6 fusion.10
  548.3 24.2 fusion.45
  572.5 3.7 gather_fusion.2
  576.2 4.9 exponential_reduce_fusion
  582.7 7.4 convert_reduce_fusion
  590.2 29.0 fusion.26
  619.2 128.3 %reshape.412 = f32[19054592]{0:T(1024)} reshape(f32[2048,9304]{1,0:T(8,128)} %fusion.26) | data formatting | bytes 152436736 | tf_op jit(solution)/shard_map/reshape | solution.py:134
  747.5 18.4 convert_reduce_fusion.1
  765.9 4.1 convolution_bitcast_fusion
  770.1 7.7 copy.110
  777.8 2.6 convert_reduce_fusion.2
  781.1 2.5 copy.109
  783.7 726.9 %concatenate.3 = f32[24166400]{0:T(1024)} concatenate(f32[901120]{0:T(1024)} %bitcast.79, f32[2048]{0:T(1024)S(1)} %get-tuple-element.65, f32[4194304]{0:T(1024)} %bitcast.77, f32[2048]{0:T(1024)S(1)} %get-tuple-element.67, f32[19054592]{0:T(1024)} %reshape.412, f32[9304]{0:T(1024)S(1)} %get-tuple-element.56, f32[2984]{0:T(1024)S(1)} %broadcast_in_dim.52), dimensions={0} | concatenate | bytes 193331200 | tf_op jit(solution)/shard_map/concatenate | solution.py:134
  1510.6 102.8 %reshape.413 = f32[47200,512]{1,0:T(8,128)} reshape(f32[24166400]{0:T(1024)} %concatenate.3) | data formatting | bytes 193331200 | tf_op jit(solution)/shard_map/reshape | solution.py:134
  1613.3 93.1 %copy.87 = f32[47200,512]{0,1:T(8,128)} copy(f32[47200,512]{1,0:T(8,128)} %reshape.413) | data formatting | bytes 193331200 | tf_op jit(solution)/shard_map/reshape | solution.py:134
  1708.3 2.5 copy.93
  1710.8 4.5 copy.83
  1715.3 2.3 copy.84
  1717.7 3.5 copy.91
  1722.5 2.3 constant_dynamic-slice_fusion.1
  1724.8 1586.0 %all-reduce.5.cloned.1.call-done = f32[47200,512]{0,1:T(8,128)} async-done(((f32[47200,512]{0,1:T(8,128)}), f32[47200,512]{0,1:T(8,128)}) %all-reduce.5.cloned.1.call-update) | async-done | bytes 96665616
  3310.8 24.5 select_multiply_fusion.1
  3335.2 30.9 reshape.475
  3366.1 12.5 reduce_sum.152
  3378.7 14.3 all_gather.14
  3393.1 7.2 multiply_reduce_fusion
  3401.7 41.5 %all-reduce.2 = (f32[]{:T(128)}, f32[]{:T(128)}) all-reduce(f32[]{:T(128)} %get-tuple-element.40, f32[]{:T(128)} %multiply_reduce_fusion.1), channel_id=1, replica_groups=mesh['node'=4,'wide'=8] {'node','wide'}, use_global_device_ids=true, to_apply=%region_8.9 | all-reduce | flops 2 | bytes 16 | tf_op jit(solution)/shard_map/psum | solution.py:123
  3448.2 8.6 convert_bitcast_fusion
  3456.8 2.6 copy.94
  3459.9 3.3 gather_fusion.1
  3464.7 12.6 mul.135
  3477.3 19.5 mul.136
  3496.9 24.6 copy.95
  3521.5 33.0 fusion
  3554.5 24.4 copy.99
  3578.9 3.5 copy.100
  3582.4 3.6 copy.96
  3586.0 4.8 copy.97
  3590.8 2.7 copy.98
  3593.5 132.1 %all-gather.11.cloned.1.call-done = bf16[32,1475,512]{2,1,0:T(8,128)(2,1)} async-done(((bf16[1,1475,512]{2,1,0:T(8,128)(2,1)}), bf16[32,1475,512]{2,1,0:T(8,128)(2,1)}) %all-gather.11.cloned.1.call-update) | async-done | bytes 48332816 | tf_op jit(solution)/shard_map/all_gather | solution.py:170
  3725.6 49.3 %reshape.470 = bf16[47200,512]{1,0:T(8,128)(2,1)} reshape(bf16[32,1475,512]{2,1,0:T(8,128)(2,1)} %all-gather.11.cloned.1.call-done) | data formatting | bytes 96665600
  3775.6 24.9 slice.78
  3800.6 8.9 slice.76
  3809.5 2.3 reshape.416
  3811.8 115.9 %reshape.418 = bf16[2048,9304]{1,0:T(8,128)(2,1)} reshape(bf16[37216,512]{1,0:T(8,128)(2,1)} %slice.78) | data formatting | bytes 76218368 | tf_op jit(solution)/shard_map/reshape | solution.py:45
  3927.8 13.9 reshape.417
  3941.7 43.5 %reshape.419 = bf16[24166400]{0:T(1024)(128)(2,1)} reshape(bf16[32,1475,512]{2,1,0:T(8,128)(2,1)} %all-gather.11.cloned.1.call-done) | data formatting | bytes 96665600 | tf_op jit(solution)/shard_map/reshape | solution.py:39
  3986.4 24.6 fusion.46
  4011.1 3.0 exponential_reduce_fusion.1
  4014.1 2.2 gather_fusion.3
  4017.0 38.7 all-reduce.1
  (120 shorter events, 18.8 us)
Async XLA Ops:
  7.2 272.9 %all-gather.7.cloned.1.call-start = ((), (), s32[]{:S(2)}) async-start(), calls=%async_computation | async-start | bytes 50012160 | tf_op jit(solution)/shard_map/all_gather | solution.py:114
  10.4 1712.0 %all-gather.9.cloned.1.call-start = ((), (), s32[]{:S(2)}) async-start(), calls=%async_computation.1 | async-start | bytes 6856704 | tf_op jit(solution)/shard_map/all_gather | solution.py:148
  35.2 11.7 copy-start.25
  35.2 12.4 copy-start.16
  46.9 3263.9 %all-reduce.5.cloned.1.call-start = ((), (), s32[]{:S(2)}) async-start(), calls=%async_computation.3 | async-start | bytes 193462272
  47.0 0.7 copy-start.20
  47.8 6.0 copy-start.18
  47.8 6.1 copy-start.19
  53.8 487.2 %copy-start.12 = (bf16[256,440]{1,0:T(8,128)(2,1)}, bf16[256,440]{1,0:T(8,128)(2,1)S(1)}, u32[]{:S(2)}) copy-start(bf16[256,440]{1,0:T(8,128)(2,1)S(1)} %reshape.400) | copy-start | bytes 675844
  339.6 25.1 slice-start
  541.0 4.7 copy-start.4
  543.6 4.8 copy-start.9
  548.3 24.2 copy-start.7
  576.2 6.5 copy-start
  582.7 7.4 copy-start.8
  765.9 11.9 slice-start.2
  770.0 7.8 slice-start.3
  770.1 7.8 copy-start.10
  777.8 2.7 copy-start.13
  1706.4 1.9 copy-start.3
  1706.5 2019.2 %all-gather.11.cloned.1.call-start = ((), (), s32[]{:S(2)}) async-start(), calls=%async_computation.2 | async-start | bytes 50012160 | tf_op jit(solution)/shard_map/all_gather | solution.py:170
  1710.8 4.5 copy-start.6
  1715.3 5.9 copy-start.26
  3378.7 14.3 copy-start.14
  3445.4 1.9 copy-start.1
  3445.4 2.8 copy-start.2
  3448.2 11.2 copy-start.21
  3448.2 11.5 copy-start.17
  3456.8 7.3 copy-start.23
  3800.6 8.9 slice-start.1
  3941.7 44.2 %copy-start.11 = (bf16[440,2048]{1,0:T(8,128)(2,1)S(1)}, bf16[440,2048]{1,0:T(8,128)(2,1)}, u32[]{:S(2)}) copy-start(bf16[440,2048]{1,0:T(8,128)(2,1)} %reshape.416) | copy-start | bytes 5406724
  3941.7 44.2 %copy-start.15 = (bf16[128,440]{1,0:T(8,128)(2,1)S(1)}, bf16[128,440]{1,0:T(8,128)(2,1)}, u32[]{:S(2)}) copy-start(bf16[128,440]{1,0:T(8,128)(2,1)} %reshape.406) | copy-start | bytes 337924
  4011.0 3.1 copy-start.5
  4011.0 5.3 copy-start.22
  4011.0 5.3 copy-start.24
Sparse Core Ops, SparseCore 0:
  11.4 268.5 all-gather.6
  282.2 61.2 all-gather.8
  1706.6 1604.1 all-reduce.4
  3459.6 266.0 all-gather.10
where the time goes:
time: 4140 us; the launch traced here: 4070 us
  waiting for transfers between devices  1940 us (47%)
  local copies, waits for them, and re-layouts  1770 us (43%)
  other arithmetic  123 us (3%)
  matrix products  109 us (3%)
  blocking collectives  94.5 us (2%)
    unnamed x5, waiting for transfers between devices  1590 us
    concatenate x1, local copies, waits for them, and re-layouts, body(): jnp.concatenate([piece.reshape(-1) for piece in pieces] + [filler])  727 us
    reshape x6, local copies, waits for them, and re-layouts, unpack(): pieces.append(line[start:start + length].reshape(shape))  265 us
    all_gather x1, waiting for transfers between devices, body(): lax.all_gather(master.astype(jnp.bfloat16), ('node', 'wide'), axis=0, til...  226 us
    unnamed x84, local copies, waits for them, and re-layouts  197 us
    reshape x2, local copies, waits for them, and re-layouts, body(): jnp.concatenate([piece.reshape(-1) for piece in pieces] + [filler])  196 us
    all_gather x1, waiting for transfers between devices, body(): lax.all_gather(average_new.astype(jnp.bfloat16), ('node', 'wide'), axis=0...  132 us
    reshape x1, local copies, waits for them, and re-layouts, body(): piece.reshape(-1)  128 us
  transfers between devices with their start and end apart: 4, of which 3 were waited for; matrix products, arithmetic and copies ran while one was open for 40% of the time, Pallas kernels for 0%

commit v1 on v0

v1 whole, which is shorter than its diff:
```python
import functools

import jax
import jax.numpy as jnp
from jax import lax
from jax.experimental import pallas as pl
from jax.experimental.pallas import tpu as pltpu
from jax.sharding import PartitionSpec as P

CONTEXT = 11
UNITS = 2048
SENONES = 9304
D_IN = 440
STEP_COUNT = 8
LANES = 128
PERIOD = 16
PERIOD_GROUPS = PERIOD * SENONES // LANES
TILES = -(-SENONES // LANES)
HEAD_ROWS = D_IN + 1 + UNITS + 1
HEAD_GROUPS = HEAD_ROWS * UNITS // LANES
TURN_TILES = 80
BLOCK = 104

CLIP_NORM = 1.0
LEARN_RATE = 0.02
BETA_ONE = 0.5
BETA_TWO = 0.5
DECAY = 0.1
AVG_KEEP = 0.9
EPS_ADAM = 1e-08


def stack_frames(feats, lengths):
    count = feats.shape[0]
    ends = jnp.cumsum(lengths)
    starts = ends - lengths
    where_t = jnp.arange(count, dtype=jnp.int32)[:, None]
    inside = (where_t >= starts[None, :]) & (where_t < ends[None, :])
    first = jnp.sum(jnp.where(inside, starts[None, :], 0), axis=1)
    last = jnp.sum(jnp.where(inside, ends[None, :], 0), axis=1) - 1
    offsets = jnp.arange(CONTEXT, dtype=jnp.int32) - CONTEXT // 2
    index = jnp.clip(where_t + offsets[None, :], first[:, None], last[:, None])
    return feats[index].reshape(count, CONTEXT * feats.shape[1])


def tile_width(tile):
    return min(LANES, SENONES - tile * LANES)


def unfold_kernel(flat_ref, out_ref, wide_ref, turn_ref):
    groups = flat_ref.shape[0]
    steps = groups // LANES

    def widen(step, carry):
        at = pl.multiple_of(step * LANES, LANES)
        wide_ref[pl.ds(at, LANES), :] = flat_ref[pl.ds(at, LANES), :].astype(jnp.float32)
        return carry

    lax.fori_loop(0, steps, widen, 0)
    tail = groups - steps * LANES
    if tail:
        wide_ref[pl.ds(steps * LANES, tail), :] = flat_ref[pl.ds(steps * LANES, tail), :].astype(jnp.float32)
    lane = lax.broadcasted_iota(jnp.int32, (TURN_TILES, LANES), 1)

    def period(step, carry):
        base = step * PERIOD_GROUPS
        for i in range(PERIOD):
            group, shift = divmod(SENONES * i, LANES)
            value = wide_ref[pl.ds(base + group, TURN_TILES), :]
            if shift:
                following = wide_ref[pl.ds(base + group + 1, TURN_TILES), :]
                value = pltpu.roll(jnp.where(lane >= shift, value, following), LANES - shift, 1)
            turn_ref[pl.ds(i, TURN_TILES, stride=PERIOD), :] = value
        rows = pl.ds(pl.multiple_of(step * PERIOD, PERIOD), PERIOD)
        for tile in range(TILES):
            width = tile_width(tile)
            piece = turn_ref[pl.ds(tile * PERIOD, PERIOD), :].astype(jnp.bfloat16)
            out_ref[rows, pl.ds(tile * LANES, width)] = piece[:, :width]
        return carry

    lax.fori_loop(0, out_ref.shape[0] // PERIOD, period, 0)


def unfold(flat):
    span = PERIOD * PERIOD
    groups = PERIOD * PERIOD_GROUPS
    return pl.pallas_call(
        unfold_kernel,
        grid=(UNITS // span,),
        out_shape=jax.ShapeDtypeStruct((UNITS, SENONES), jnp.bfloat16),
        in_specs=[
            pl.BlockSpec((pl.Element(groups), pl.Element(LANES)), lambda m: (PERIOD * (HEAD_GROUPS // PERIOD + PERIOD_GROUPS * m), 0))
        ],
        out_specs=pl.BlockSpec((span, SENONES), lambda m: (m, 0)),
        scratch_shapes=[
            pltpu.VMEM((groups + TURN_TILES + 16, LANES), jnp.float32),
            pltpu.VMEM((TURN_TILES * PERIOD, LANES), jnp.float32),
        ],
    )(flat)


def unpack(flat):
    head = flat[:HEAD_GROUPS].reshape(HEAD_ROWS, UNITS)
    w_in = head[:D_IN]
    b_in = head[D_IN]
    w_mid = head[D_IN + 1 : D_IN + 1 + UNITS]
    b_mid = head[D_IN + 1 + UNITS]
    at = HEAD_GROUPS + UNITS * SENONES // LANES
    b_out = flat[at : at + TILES].reshape(-1)[:SENONES]
    return (w_in, b_in, w_mid, b_mid, unfold(flat), b_out)


def gather_flat(block):
    rows = block.shape[0] * block.shape[1] // LANES
    low = block.astype(jnp.bfloat16).reshape(rows, LANES)
    return lax.all_gather(low, ("node", "wide"), axis=0, tiled=True)


def layer_forward(inputs, weight, bias):
    return jnp.dot(inputs, weight, preferred_element_type=jnp.float32) + bias.astype(jnp.float32)


def contract_rows(left, right):
    return lax.dot_general(left, right, (((0,), (0,)), ((), ())), preferred_element_type=jnp.float32)


def contract_columns(left, right):
    return lax.dot_general(left, right, (((1,), (1,)), ((), ())), preferred_element_type=jnp.float32)


def run_layers(params, stacked):
    w_in, b_in, w_mid, b_mid, w_out, b_out = params
    sig_one = jax.nn.sigmoid(layer_forward(stacked, w_in, b_in))
    h_one = sig_one.astype(jnp.bfloat16)
    sig_two = jax.nn.sigmoid(layer_forward(h_one, w_mid, b_mid))
    h_two = sig_two.astype(jnp.bfloat16)
    logits = layer_forward(h_two, w_out, b_out)
    return (sig_one, h_one, sig_two, h_two, logits)


def frame_terms(logits, labels, weights):
    hit = labels[:, None] == lax.broadcasted_iota(jnp.int32, logits.shape, 1)
    top = jnp.max(logits, axis=1)
    total = jnp.sum(jnp.exp(logits - top[:, None]), axis=1)
    picked = jnp.sum(jnp.where(hit, logits, 0.0), axis=1)
    lse = jnp.log(total) + top
    return (jnp.sum(weights * (lse - picked)), lse, hit)


def pack_signs(rest):
    bits = (rest >= 0).astype(jnp.int32).reshape(rest.shape[0], rest.shape[1] // 32, 32)
    shifts = jnp.arange(32, dtype=jnp.int32)
    return jnp.sum(jnp.left_shift(bits, shifts), axis=2)


def unpack_signs(words):
    shifts = jnp.arange(32, dtype=jnp.int32)
    bits = jnp.bitwise_and(jnp.right_shift(words[..., None], shifts), 1)
    signs = (2 * bits - 1).astype(jnp.float32)
    return signs.reshape(words.shape[:-1] + (words.shape[-1] * 32,))


def padded(values, columns):
    count = values.shape[0]
    one = jnp.ones((count, 1), jnp.bfloat16)
    rest = jnp.zeros((count, columns - values.shape[1] - 1), jnp.bfloat16)
    return jnp.concatenate([values, one, rest], axis=1)


def code_kernel(plan, offset_ref, *refs):
    grad_refs = refs[: plan["inputs"]]
    residual_ref, new_ref, scale_ref, flat_ref, turn_ref, sum_ref = refs[plan["inputs"] :]
    step = pl.program_id(0)
    head, body, chunks = plan["head"], plan["body"], plan["chunks"]
    chunk, shard, margin, overlap = plan["chunk"], plan["shard"], plan["margin"], plan["overlap"]
    count = sum_ref.shape[0] // 8
    per_row = residual_ref.shape[1] // LANES
    if head:

        def place(ref, row):
            for tile in range(UNITS // LANES):
                at = row * (UNITS // LANES) + tile
                flat_ref[pl.ds(at, BLOCK, stride=UNITS // LANES), :] = ref[:, pl.ds(tile * LANES, LANES)]

        split = plan["split"]

        @pl.when(step < split)
        def _():
            place(grad_refs[0], step * BLOCK)

        @pl.when((step >= split) & (step < head))
        def _():
            place(grad_refs[1], D_IN + 1 + (step - split) * BLOCK)

    out_grad = grad_refs[-1]

    @pl.when((step >= head) & (step < head + body))
    def _():
        base = offset_ref[0] + (step - head) * PERIOD_GROUPS
        for tile in range(TILES):
            width = tile_width(tile)
            turn_ref[pl.ds((tile + 1) * PERIOD, PERIOD), pl.ds(0, width)] = out_grad[:, pl.ds(tile * LANES, width)]
        lane = lax.broadcasted_iota(jnp.int32, (TURN_TILES, LANES), 1)
        row = lax.broadcasted_iota(jnp.int32, (TURN_TILES, LANES), 0)
        for i in range(PERIOD):
            group, shift = divmod(SENONES * i, LANES)
            value = turn_ref[pl.ds(PERIOD + i, TURN_TILES, stride=PERIOD), :]
            at = pl.ds(base + group, TURN_TILES)
            if shift:
                before = turn_ref[pl.ds(i, TURN_TILES, stride=PERIOD), :]
                value = pltpu.roll(jnp.where(lane < LANES - shift, value, before), shift, 1)
                value = jnp.where((row == 0) & (lane < shift), flat_ref[at, :], value)
            flat_ref[at, :] = value

    second = head + body
    lane_row = lax.broadcasted_iota(jnp.int32, (8, LANES), 0)

    @pl.when(step == second)
    def _():
        sum_ref[...] = jnp.zeros_like(sum_ref)

    @pl.when((step >= second) & (step < second + chunks))
    def _():
        index = step - second
        first = index * chunk // shard
        start = margin + per_row * chunk * index
        totals = [[jnp.zeros((8, LANES), jnp.float32) for _ in range(per_row)] for _ in range(overlap)]
        for i in range(chunk // 8):
            rows = lane_row + (index * chunk + 8 * i)
            inside = [
                (rows >= (first + j) * shard) & (rows < (first + j + 1) * shard) for j in range(overlap)
            ]
            for tile in range(per_row):
                at = pl.ds(start + per_row * 8 * i + tile, 8, stride=per_row)
                rest = residual_ref[pl.ds(8 * i, 8), pl.ds(tile * LANES, LANES)]
                value = flat_ref[at, :] + rest
                flat_ref[at, :] = value
                signed = jnp.where(rest >= 0, value, -value)
                for j in range(overlap):
                    totals[j][tile] = totals[j][tile] + jnp.where(inside[j], signed, 0.0)
        for j in range(overlap):

            @pl.when(first + j < count)
            def _():
                at = pl.ds(pl.multiple_of((first + j) * 8, 8), 8)
                for tile in range(per_row):
                    columns = pl.ds(tile * LANES, LANES)
                    sum_ref[at, columns] = sum_ref[at, columns] + totals[j][tile]

    third = second + chunks

    @pl.when(step == third)
    def _():
        for block in range(count):
            total = jnp.sum(sum_ref[pl.ds(8 * block, 8), :], axis=0, keepdims=True)
            mean = total / shard
            sum_ref[pl.ds(8 * block, 8), :] = jnp.broadcast_to(mean, (8, mean.shape[1]))
            scale_ref[pl.ds(block, 1), :] = mean

    @pl.when(step >= third)
    def _():
        index = step - third
        first = index * chunk // shard
        start = margin + per_row * chunk * index
        scales = []
        for j in range(overlap):
            at = pl.ds(pl.multiple_of(jnp.minimum(first + j, count - 1) * 8, 8), 8)
            scales.append([sum_ref[at, pl.ds(tile * LANES, LANES)] for tile in range(per_row)])
        for i in range(chunk // 8):
            rows = lane_row + (index * chunk + 8 * i)
            for tile in range(per_row):
                scale = scales[0][tile]
                for j in range(1, overlap):
                    scale = jnp.where(rows >= (first + j) * shard, scales[j][tile], scale)
                at = pl.ds(start + per_row * 8 * i + tile, 8, stride=per_row)
                columns = pl.ds(tile * LANES, LANES)
                rest = residual_ref[pl.ds(8 * i, 8), columns]
                coded = jnp.where(rest >= 0, scale, -scale)
                new_ref[pl.ds(8 * i, 8), columns] = flat_ref[at, :] - coded


def code(grads, offset, residual, shard, margin):
    quarter, width = residual.shape
    count = quarter // shard
    tiles = quarter // 8
    chunk = 8 * max(f for f in range(1, 65) if tiles % f == 0)
    chunks = quarter // chunk
    overlap = (chunk - 1 + shard - 1) // shard + 1
    body = grads[-1].shape[0] // PERIOD
    split = grads[0].shape[0] // BLOCK if len(grads) > 1 else 0
    head = split + (grads[1].shape[0] // BLOCK if len(grads) > 1 else 0)
    third = head + body + chunks
    plan = dict(
        inputs=len(grads), head=head, split=split, body=body, chunk=chunk, chunks=chunks,
        shard=shard, margin=margin, overlap=overlap,
    )
    groups = margin + quarter * width // LANES

    def residual_map(s, _):
        return (jnp.where(s >= third, s - third, jnp.clip(s - head - body, 0, chunks - 1)), 0)

    specs = []
    if head:
        specs.append(pl.BlockSpec((BLOCK, UNITS), lambda s, _: (jnp.minimum(s, split - 1), 0)))
        specs.append(pl.BlockSpec((BLOCK, UNITS), lambda s, _: (jnp.clip(s - split, 0, head - split - 1), 0)))
    specs.append(pl.BlockSpec((PERIOD, SENONES), lambda s, _: (jnp.clip(s - head, 0, body - 1), 0)))
    specs.append(pl.BlockSpec((chunk, width), residual_map))
    return pl.pallas_call(
        functools.partial(code_kernel, plan),
        out_shape=(
            jax.ShapeDtypeStruct(residual.shape, jnp.float32),
            jax.ShapeDtypeStruct((count, width), jnp.float32),
        ),
        grid_spec=pltpu.PrefetchScalarGridSpec(
            num_scalar_prefetch=1,
            grid=(third + chunks,),
            in_specs=specs,
            out_specs=(
                pl.BlockSpec((chunk, width), lambda s, _: (jnp.maximum(s - third, 0), 0)),
                pl.BlockSpec((count, width), lambda s, _: (0, 0)),
            ),
            scratch_shapes=[
                pltpu.VMEM((groups + 3 * PERIOD_GROUPS, LANES), jnp.float32),
                pltpu.VMEM(((TURN_TILES + 1) * PERIOD, LANES), jnp.float32),
                pltpu.VMEM((8 * count, width), jnp.float32),
            ],
        ),
    )(offset, *grads, residual)


def body(
    feats,
    utt_lengths,
    frame_mask,
    targets,
    val_feats,
    val_mask,
    val_targets,
    master,
    first_moment,
    second_moment,
    residual,
    average,
):
    width = master.shape[1]
    shard_rows = master.shape[0]
    quarter_rows = residual.shape[0]
    wide_count = lax.axis_size("wide")
    node_count = lax.axis_size("node")
    node_at = lax.axis_index("node")
    wide_at = lax.axis_index("wide")
    params = unpack(gather_flat(master))
    w_in, b_in, w_mid, b_mid, w_out, b_out = params
    words = pack_signs(residual)
    all_words = lax.all_gather(words, "wide", axis=0, tiled=True).reshape(
        wide_count, quarter_rows, width // 32
    )
    own_words = lax.dynamic_slice_in_dim(all_words, wide_at * shard_rows, shard_rows, 1)
    stacked = lax.all_gather(stack_frames(feats, utt_lengths[0]), "node", axis=0, tiled=True)
    marks = lax.all_gather(jnp.stack([targets, frame_mask]), "node", axis=1, tiled=True)
    labels = marks[0]
    weights = marks[1].astype(jnp.float32)
    sig_one, h_one, sig_two, h_two, logits = run_layers(params, stacked)
    loss_part, lse, hit = frame_terms(logits, labels, weights)
    probs = jnp.exp(logits - lse[:, None])
    delta_out = (weights[:, None] * jnp.where(hit, probs - 1.0, probs)).astype(jnp.bfloat16)

    row_groups = width // LANES
    quarter_groups = quarter_rows * row_groups
    starts = []
    offsets = []
    lengths = []
    for node in range(node_count):
        begin = node * quarter_groups - HEAD_GROUPS
        start = max(begin, 0) * LANES // SENONES // PERIOD * PERIOD
        stop = -(-(begin + quarter_groups) * LANES // SENONES)
        starts.append(start)
        lengths.append(-(-(stop - start) // PERIOD) * PERIOD)
        offsets.append(start * SENONES // LANES - begin)
    margin = PERIOD_GROUPS + 5

    def first_quarter(_):
        back_two = contract_columns(delta_out, w_out)
        delta_two = (back_two * (sig_two * (1.0 - sig_two))).astype(jnp.bfloat16)
        back_one = contract_columns(delta_two, w_mid)
        delta_one = (back_one * (sig_one * (1.0 - sig_one))).astype(jnp.bfloat16)
        g_in = contract_rows(padded(stacked, -(-(D_IN + 1) // BLOCK) * BLOCK), delta_one)
        g_mid = contract_rows(padded(h_one, -(-(UNITS + 1) // BLOCK) * BLOCK), delta_two)
        g_out = contract_rows(h_two[:, : lengths[0]], delta_out)
        offset = jnp.full((1,), offsets[0], jnp.int32)
        return code((g_in, g_mid, g_out), offset, residual, shard_rows, 0)

    def other_quarter(_):
        span = max(lengths[1:])
        begin = jnp.asarray(starts, jnp.int32)[node_at]
        offset = jnp.asarray(offsets, jnp.int32)[node_at] + margin
        longest = max(start + span for start in starts)
        extended = padded(h_two, -(-longest // LANES) * LANES)
        picked = lax.dynamic_slice_in_dim(extended, begin, span, 1)
        g_out = contract_rows(picked, delta_out)
        return code((g_out,), offset[None], residual, shard_rows, margin)

    residual_new, scales = lax.cond(node_at == 0, first_quarter, other_quarter, 0)
    loss_sum, count = lax.psum((loss_part, jnp.sum(weights)), "wide")
    all_scales = lax.all_gather(scales, "wide", axis=0, tiled=True).reshape(
        wide_count, wide_count, width
    )
    own_scales = lax.dynamic_index_in_dim(all_scales, wide_at, 1, keepdims=False)
    decoded = jnp.sum(unpack_signs(own_words) * own_scales[:, None, :], axis=0)
    square_part = jnp.sum(decoded * decoded)
    square_sum = lax.psum(square_part, ("node", "wide"))
    grad_norm = jnp.sqrt(square_sum) / count
    factor = jnp.minimum(1.0, CLIP_NORM / (grad_norm + 1e-06))
    grad = decoded * (factor / count)
    first_new = BETA_ONE * first_moment + (1.0 - BETA_ONE) * grad
    second_new = BETA_TWO * second_moment + (1.0 - BETA_TWO) * grad * grad
    first_hat = first_new / (1.0 - BETA_ONE**STEP_COUNT)
    second_hat = second_new / (1.0 - BETA_TWO**STEP_COUNT)
    master_new = master - LEARN_RATE * (
        first_hat / (jnp.sqrt(second_hat) + EPS_ADAM) + DECAY * master
    )
    average_new = AVG_KEEP * average + (1.0 - AVG_KEEP) * master_new
    val_params = unpack(gather_flat(average_new))
    val_stacked = stack_frames(val_feats, jnp.full((1,), val_feats.shape[0], jnp.int32))
    val_logits = run_layers(val_params, val_stacked)[4]
    val_weights = val_mask.astype(jnp.float32)
    val_part = frame_terms(val_logits, val_targets, val_weights)[0]
    val_sum, val_count = lax.psum((val_part, jnp.sum(val_weights)), ("node", "wide"))
    return (
        loss_sum / count,
        val_sum / val_count,
        grad_norm,
        master_new,
        first_new,
        second_new,
        residual_new,
        average_new,
    )


def solution(mesh):
    return jax.shard_map(
        body,
        mesh=mesh,
        in_specs=(
            P(("node", "wide"), None),
            P(("node", "wide"), None),
            P(("node", "wide")),
            P(("node", "wide")),
            P(("node", "wide"), None),
            P(("node", "wide")),
            P(("node", "wide")),
            P(("node", "wide"), None),
            P(("node", "wide"), None),
            P(("node", "wide"), None),
            P(("node", "wide"), None),
            P(("node", "wide"), None),
        ),
        out_specs=(
            P(),
            P(),
            P(),
            P(("node", "wide"), None),
            P(("node", "wide"), None),
            P(("node", "wide"), None),
            P(("node", "wide"), None),
            P(("node", "wide"), None),
        ),
        check_vma=False,
    )
```

time: 4140 us -> 1380 us (0.33); the launches traced: 4070 us -> 1360 us
  local copies, waits for them, and re-layouts: 1770 us -> 206 us
  waiting for transfers between devices: 1940 us -> 530 us
  Pallas kernels: 0 us -> 204 us
  matrix products: 109 us -> 193 us
  other arithmetic: 123 us -> 79.5 us
    unnamed x5 -> x3, waiting for transfers between devices: 1590 us -> 0.05 us
    concatenate x1 -> x2, local copies, waits for them, and re-layouts: 727 us -> 7.81 us  [padded(): return jnp.concatenate([values, one, rest], axis=1)]
    reshape x12 -> x2, local copies, waits for them, and re-layouts: 706 us -> 1.46 us  [unpack(): b_out = flat[at:at + TILES].reshape(-1)[:SENONES]]
    pallas_call x0 -> x3, Pallas kernels: none -> 204 us  [the longest x2 128 us: unfold(): pl.pallas_call(unfold_kernel, grid=(UNITS // span,), out_shape=jax.ShapeD...]
    all_gather x2, waiting for transfers between devices: 358 us -> 509 us  [gather_flat(): return lax.all_gather(low, ('node', 'wide'), axis=0, tiled=True)]
    unnamed x84 -> x55, local copies, waits for them, and re-layouts: 197 us -> 136 us
    mul x3 -> x0, local copies, waits for them, and re-layouts: 56.7 us -> none  [body(): signs.reshape(wide_count, shard_rows, width) * scales[:, None, :]]
    dot_general x5 -> x4, matrix products: 54.8 us -> 99 us  [the longest x1 51.2 us: contract_columns(): lax.dot_general(left, right, (((1,), (1,)), ((), ())), preferred_element_...]
  transfers between devices with their start and end apart: 4 -> 3, of which waited for: 3 -> 3; matrix products, arithmetic and copies ran while one was open for 40% -> 3% of each run, Pallas kernels for 0% -> 0%
where the time goes in v1:
time: 1380 us; the launch traced here: 1360 us
  waiting for transfers between devices  530 us (38%)
  local copies, waits for them, and re-layouts  206 us (15%)
  Pallas kernels  204 us (15%)
  matrix products  193 us (14%)
  blocking collectives  128 us (9%)
  other arithmetic  79.5 us (6%)
  between operations  22.3 us (2%)
    all_gather x2, waiting for transfers between devices, gather_flat(): return lax.all_gather(low, ('node', 'wide'), axis=0, tiled=True)  509 us
    unnamed x55, local copies, waits for them, and re-layouts  136 us
    pallas_call x2, Pallas kernels, unfold(): pl.pallas_call(unfold_kernel, grid=(UNITS // span,), out_shape=jax.ShapeD...  128 us
    dot_general x5, matrix products, layer_forward(): jnp.dot(inputs, weight, preferred_element_type=jnp.float32)  93.9 us
    pallas_call x1, Pallas kernels, code(): pl.pallas_call(functools.partial(code_kernel, plan), out_shape=(jax.Shape...  75.1 us
    dot_general x1, matrix products, contract_columns(): lax.dot_general(left, right, (((1,), (1,)), ((), ())), preferred_element_...  51.2 us
    dot_general x3, matrix products, contract_rows(): lax.dot_general(left, right, (((0,), (0,)), ((), ())), preferred_element_...  47.8 us
    slice x4, local copies, waits for them, and re-layouts, unpack(): w_mid = head[D_IN + 1:D_IN + 1 + UNITS]  41.2 us
  transfers between devices with their start and end apart: 3, of which 3 were waited for; matrix products, arithmetic and copies ran while one was open for 3% of the time, Pallas kernels for 0%

profile of v1, /device:TPU:0, one launch (start us, length us, event | category | flops | bytes accessed | tf_op | source)
XLA Modules:
  0.0 1363.5 jit_solution(11703540832849731412)
XLA Ops:
  7.2 24.5 %copy.79 = f32[11800,512]{0,1:T(8,128)} copy(f32[11800,512]{1,0:T(8,128)} %param.26) | data formatting | bytes 48332800 | tf_op args[10]
  31.7 11.7 shift-left_reduce_fusion
  43.5 1.3 convert_element_type.97
  44.8 3.6 reshape.359
  48.5 2.4 copy.84
  51.7 5.6 gather_fusion
  57.8 3.6 copy.77
  61.4 3.5 copy.78
  64.9 9.5 all_gather.18
  74.5 0.6 fusion.41
  75.1 13.1 all_gather.19
  88.2 0.6 fusion.44
  88.8 20.6 %all-gather.9.cloned.1.call-done = s32[8,11800,16]{1,2,0:T(8,128)} async-done(((s32[1,11800,16]{1,2,0:T(8,128)}), s32[8,11800,16]{1,2,0:T(8,128)}) %all-gather.9.cloned.1.call-update) | async-done | bytes 6041616 | tf_op jit(solution)/shard_map/all_gather | solution.py:355
  109.4 2.3 constant_dynamic-slice_fusion
  111.7 265.3 %all-gather.7.cloned.1.call-done = bf16[32,5900,128]{2,1,0:T(8,128)(2,1)} async-done(((bf16[1,5900,128]{2,1,0:T(8,128)(2,1)}), bf16[32,5900,128]{2,1,0:T(8,128)(2,1)}) %all-gather.7.cloned.1.call-update) | async-done | bytes 48332816 | tf_op jit(solution)/shard_map/all_gather | solution.py:116
  377.0 37.6 %reshape.360.flat_ref = bf16[188800,128]{1,0:T(8,128)(2,1)} reshape(bf16[32,5900,128]{2,1,0:T(8,128)(2,1)} %all-gather.7.cloned.1.call-done) | data formatting | bytes 96665600
  414.6 0.7 fusion.37
  415.3 7.1 slice.96
  422.4 0.7 slice_bitcast_fusion.1
  423.1 64.4 %shard_map.201 = bf16[2048,9304]{1,0:T(8,128)(2,1)} custom-call(bf16[188800,128]{1,0:T(8,128)(2,1)} %reshape.360.flat_ref), custom_call_target="tpu_custom_call" | custom-call | tf_op jit(solution)/shard_map/pallas_call | solution.py:87
  487.5 2.0 slice.73
  489.5 13.4 slice.76
  502.9 5.3 fusion.45
  508.2 11.9 fusion.46
  520.1 51.3 %add_reduce_fusion = (f32[1024]{0:T(1024)S(1)}, f32[1024,9304]{0,1:T(8,128)}) fusion(f32[9304]{0:T(1024)S(1)} %slice_convert_fusion.1, bf16[1024,2048]{1,0:T(8,128)(2,1)S(1)} %get-tuple-element.193, bf16[2048,9304]{1,0:T(8,128)(2,1)} %shard_map.201), kind=kOutput, calls=%fused_computation.28 | convolution fusion | flops 39042859008 | bytes 80453984 | tf_op jit(solution)/shard_map/dot_general | solution.py:120
  571.5 17.7 %select_reduce_fusion = (f32[1024]{0:T(1024)S(1)}, f32[1024]{0:T(1024)S(1)}) fusion(f32[1024,9304]{0,1:T(8,128)} %get-tuple-element.196, s32[1024]{0:T(1024)S(1)} %bitcast.71, f32[9304]{0:T(1024)S(1)} %slice_convert_fusion.1, f32[1024]{0:T(1024)S(1)} %get-tuple-element.195), kind=kLoop, calls=%fused_computation.25 | loop fusion | flops 57161728 | bytes 38162784 | tf_op jit(solution)/shard_map/reduce_sum | solution.py:145
  589.1 0.6 multiply_reduce_fusion.2
  589.7 25.2 %fusion.19 = bf16[1024,9304]{0,1:T(8,128)(2,1)} fusion(f32[1024,9304]{0,1:T(8,128)} %get-tuple-element.196, f32[1024]{0:T(1024)S(1)} %get-tuple-element.184, f32[1024]{0:T(1024)S(1)} %bitcast.74, s32[1024]{0:T(1024)S(1)} %bitcast.72, f32[9304]{0:T(1024)S(1)} %slice_convert_fusion.1), kind=kLoop, calls=%fused_computation.24 | loop fusion | flops 66691072 | bytes 57213280 | tf_op jit(solution)/shard_map/convert_element_type | solution.py:366
  614.9 182.6 %conditional.1 = ((f32[11800,512]{1,0:T(8,128)}, f32[8,512]{1,0:T(8,128)S(1)})) conditional(s32[]{:T(128)} %convert_element_type.107, (s32[]{:T(128)}, bf16[1024,2048]{1,0:T(8,128)(2,1)}, bf16[1024,9304]{0,1:T(8,128)(2,1)}, f32[11800,512]{1,0:T(8,128)}) %tuple.61, (bf16[1024,440]{1,0:T(8,128)(2,1)S(1)}, bf16[1024,9304]{0,1:T(8,128)(2,1)}, ...), branch_computations={%region_11.12_spmd.clone, %region_12.13_spmd} | conditional | flops 60673015808 | bytes 153447264 | solution.py:403
  615.1 51.2 %fusion.1 = bf16[1024,2048]{1,0:T(8,128)(2,1)} fusion(f32[1024,2048]{1,0:T(8,128)} %get-tuple-element.39, bf16[1024,9304]{0,1:T(8,128)(2,1)} %get-tuple-element.150, bf16[2048,9304]{1,0:T(8,128)(2,1)} %get-tuple-element.38), kind=kOutput, calls=%fused_computation.5 | convolution fusion | flops 39032193024 | bytes 69746688 | tf_op jit(solution)/shard_map/cond/branch_1_fun/dot_general | solution.py:128
  666.4 7.7 concatenate.8
  674.1 15.6 %fusion.48.refs_1_ = f32[2080,2048]{1,0:T(8,128)} fusion(bf16[1024,2080]{1,0:T(8,128)(2,1)} %concatenate.8, bf16[1024,2048]{1,0:T(8,128)(2,1)} %fusion.1), kind=kOutput, calls=%fused_computation.101 | convolution fusion | flops 8724152320 | bytes 25493504 | tf_op jit(solution)/shard_map/cond/branch_1_fun/dot_general | solution.py:124
  689.7 17.7 %fusion.4.refs_0_ = f32[520,2048]{1,0:T(8,128)} fusion(f32[1024,2048]{1,0:T(8,128)} %get-tuple-element.41, bf16[1024,2048]{1,0:T(8,128)(2,1)} %fusion.1, bf16[2048,2048]{1,0:T(8,128)(2,1)} %get-tuple-element.40, bf16[1024,1]{1,0:T(8,128)(2,1)S(1)} %broadcast.253, bf16[1024,440]{1,0:T(8,128)(2,1)S(1)} %get-tuple-element.36, bf16[520]{0:T(1024)(128)(2,1)S(1)} %pad.2.clone), kind=kOutput, calls=%fused_computation.8 | convolution fusion | flops 10782556160 | bytes 26135568 | tf_op jit(solution)/shard_map/cond/branch_1_fun/dot_general | solution.py:124
  707.5 14.5 %fusion.11.refs_2_ = f32[112,9304]{1,0:T(8,128)} fusion(bf16[1024,9304]{0,1:T(8,128)(2,1)} %get-tuple-element.150, bf16[1024,2048]{1,0:T(8,128)(2,1)} %get-tuple-element.43), kind=kOutput, calls=%fused_computation.15 | convolution fusion | flops 2134114304 | bytes 23484928 | tf_op jit(solution)/shard_map/cond/branch_1_fun/dot_general | solution.py:124
  722.0 75.1 %branch_1_fun.1 = (f32[11800,512]{1,0:T(8,128)}, f32[8,512]{1,0:T(8,128)S(1)}) custom-call(s32[1]{0:T(128)} %constant.35.clone.offset_ref, f32[520,2048]{1,0:T(8,128)} %fusion.4.refs_0_, f32[2080,2048]{1,0:T(8,128)} %fusion.48.refs_1_, f32[112,9304]{1,0:T(8,128)} %fusion.11.refs_2_, f32[11800,512]{1,0:T(8,128)} %get-tuple-element.44.refs_3_), custom_call_target="tpu_custom_call" | custom-call | tf_op jit(solution)/shard_map/cond/branch_1_fun/pallas_call | solution.py:308
  797.5 14.0 %all_gather.22 = f32[64,512]{1,0:T(8,128)S(1)} all-gather(f32[8,512]{1,0:T(8,128)S(1)} %get-tuple-element.55), channel_id=1, replica_groups=mesh['node'=4,'wide'=8] {'wide'}, dimensions={0}, use_global_device_ids=true | all-gather | bytes 147456 | tf_op jit(solution)/shard_map/all_gather | solution.py:405
  811.6 7.2 multiply_reduce_fusion
  818.8 1.4 multiply_reduce_fusion.1
  820.2 3.5 copy.82
  823.7 37.6 %psum.37 = f32[]{:T(128)} all-reduce(f32[]{:T(128)} %multiply_reduce_fusion.1), channel_id=1, replica_groups=mesh['node'=4,'wide'=8] {'node','wide'}, use_global_device_ids=true, to_apply=%region_15.16 | all-reduce | flops 1 | bytes 8 | tf_op jit(solution)/shard_map/psum | solution.py:411
  862.1 15.3 %all-reduce.1 = (f32[]{:T(128)}, f32[]{:T(128)}) all-reduce(f32[]{:T(128)} %get-tuple-element.183, f32[]{:T(128)} %fusion.41), channel_id=1, replica_groups=mesh['node'=4,'wide'=8] {'wide'}, use_global_device_ids=true, to_apply=%region_7.8 | all-reduce | flops 2 | bytes 16 | tf_op jit(solution)/shard_map/psum | solution.py:404
  879.2 1.5 copy-done
  880.7 1.0 copy-done.1
  881.6 7.1 fusion.42
  888.8 2.6 copy.85
  891.3 3.6 reshape.363
  895.4 3.3 gather_fusion.1
  898.8 0.9 reshape.326
  899.7 3.9 copy.86
  903.6 3.9 copy.87
  907.4 3.5 copy.88
  910.9 2.3 copy.89
  914.6 244.0 %all-gather.11.cloned.1.call-done = bf16[32,5900,128]{2,1,0:T(8,128)(2,1)} async-done(((bf16[1,5900,128]{2,1,0:T(8,128)(2,1)}), bf16[32,5900,128]{2,1,0:T(8,128)(2,1)}) %all-gather.11.cloned.1.call-update) | async-done | bytes 48332816 | tf_op jit(solution)/shard_map/all_gather | solution.py:116
  1158.5 37.7 %reshape.364.flat_ref = bf16[188800,128]{1,0:T(8,128)(2,1)} reshape(bf16[32,5900,128]{2,1,0:T(8,128)(2,1)} %all-gather.11.cloned.1.call-done) | data formatting | bytes 96665600
  1196.2 0.7 fusion.34
  1196.9 64.1 %shard_map.202 = bf16[2048,9304]{1,0:T(8,128)(2,1)} custom-call(bf16[188800,128]{1,0:T(8,128)(2,1)} %reshape.364.flat_ref), custom_call_target="tpu_custom_call" | custom-call | tf_op jit(solution)/shard_map/pallas_call | solution.py:87
  1261.0 7.2 slice.103
  1268.1 0.7 slice_bitcast_fusion
  1268.9 2.0 slice.82
  1270.9 13.5 slice.85
  1285.0 24.8 %fusion.47 = (f32[128]{0:T(128)S(1)}, f32[128,9304]{0,1:T(8,128)}) fusion(f32[9304]{0:T(1024)S(1)} %slice_convert_fusion, bf16[2048,9304]{1,0:T(8,128)(2,1)} %shard_map.202, bf16[128,2048]{1,0:T(8,128)(2,1)S(1)} %fusion.29, bf16[2048,2048]{1,0:T(8,128)(2,1)} %slice.85, f32[2048]{0:T(1024)S(1)} %get-tuple-element.185), kind=kOutput, calls=%fused_computation.100 | convolution fusion | flops 5955409920 | bytes 51831648 | tf_op jit(solution)/shard_map/dot_general | solution.py:120
  1309.8 3.0 exponential_reduce_fusion.1
  1312.8 0.7 convert_reduce_fusion
  1313.5 38.6 %all-reduce = (f32[]{:T(128)}, f32[]{:T(128)}) all-reduce(f32[]{:T(128)} %get-tuple-element.173, f32[]{:T(128)} %get-tuple-element.172), channel_id=1, replica_groups=mesh['node'=4,'wide'=8] {'node','wide'}, use_global_device_ids=true, to_apply=%region_20.21 | all-reduce | flops 2 | bytes 16 | tf_op jit(solution)/shard_map/psum | solution.py:428
  (74 shorter events, 3.0 us)
Async XLA Ops:
  7.2 102.2 %all-gather.9.cloned.1.call-start = ((), (), s32[]{:S(2)}) async-start(), calls=%async_computation.1 | async-start | bytes 6856704 | tf_op jit(solution)/shard_map/all_gather | solution.py:355
  31.7 11.8 copy-start.2
  43.4 7.5 copy-start.19
  43.4 8.2 copy-start.11
  43.4 333.6 %all-gather.7.cloned.1.call-start = ((), (), s32[]{:S(2)}) async-start(), calls=%async_computation | async-start | bytes 49876992 | tf_op jit(solution)/shard_map/all_gather | solution.py:116
  48.5 1110.0 %all-gather.11.cloned.1.call-start = ((), (), s32[]{:S(2)}) async-start(), calls=%async_computation.2 | async-start | bytes 49876992 | tf_op jit(solution)/shard_map/all_gather | solution.py:116
  51.1 0.6 copy-start.13
  57.3 7.6 copy-start.15
  57.3 7.6 copy-start.16
  423.1 64.4 %slice-start = ((bf16[188800,128]{1,0:T(8,128)(2,1)}), bf16[7040,128]{1,0:T(8,128)(2,1)S(1)}, s32[]{:S(2)}) async-start(bf16[188800,128]{1,0:T(8,128)(2,1)} %reshape.360.flat_ref), calls=%async_computation.3 | async-start | bytes 3604480 | tf_op jit(solution)/shard_map/slice | solution.py:104
  489.5 13.4 copy-start.6
  502.9 5.3 copy-start.3
  508.2 11.9 copy-start.5
  520.1 51.3 %copy-start.4 = (bf16[1024,2048]{1,0:T(8,128)(2,1)}, bf16[1024,2048]{1,0:T(8,128)(2,1)S(1)}, u32[]{:S(2)}) copy-start(bf16[1024,2048]{1,0:T(8,128)(2,1)S(1)} %get-tuple-element.193) | copy-start | bytes 12582916
  520.1 51.3 %copy-start.9 = (s32[1,1024]{1,0:T(1,128)S(1)}, s32[1,1024]{1,0:T(1,128)}, u32[]{:S(2)}) copy-start(s32[1,1024]{1,0:T(1,128)} %get-tuple-element.189) | copy-start | bytes 12292
  571.5 17.7 %copy-start.10 = (f32[1,1024]{1,0:T(1,128)S(1)}, f32[1,1024]{1,0:T(1,128)}, u32[]{:S(2)}) copy-start(f32[1,1024]{1,0:T(1,128)} %get-tuple-element.190) | copy-start | bytes 12292
  878.8 1.9 copy-start
  878.8 2.8 copy-start.1
  881.6 13.4 copy-start.14
  881.6 13.7 %copy-start.12 = (bf16[128,40]{0,1:T(8,128)(2,1)S(1)}, bf16[128,40]{0,1:T(8,128)(2,1)}, u32[]{:S(2)}) copy-start(bf16[128,40]{0,1:T(8,128)(2,1)} %param.20) | copy-start | bytes 30724
  1261.0 7.9 slice-start.1
  1270.9 13.5 copy-start.7
  1270.9 13.5 copy-start.8
  1284.9 24.9 %copy-start.17 = (s32[128]{0:T(128)S(1)}, s32[128]{0:T(128)}, u32[]{:S(2)}) copy-start(s32[128]{0:T(128)} %param.22) | copy-start | bytes 1540
  1284.9 27.9 %copy-start.18 = (s32[128]{0:T(128)S(1)}, s32[128]{0:T(128)}, u32[]{:S(2)}) copy-start(s32[128]{0:T(128)} %param.21) | copy-start | bytes 1540
Sparse Core Ops, SparseCore 0:
  43.6 65.7 all-gather.8
  113.0 263.9 all-gather.6
  895.1 263.3 all-gather.10

commit v2 on v1

--- a/solution.py
+++ b/solution.py
@@ -47,28 +47,56 @@
     return min(LANES, SENONES - tile * LANES)
 
 
-def unfold_kernel(flat_ref, out_ref, wide_ref, turn_ref):
-    groups = flat_ref.shape[0]
-    steps = groups // LANES
+def window_of(step, plan):
+    base = jnp.where(
+        step == 0,
+        0,
+        jnp.where(
+            step <= plan["middle"],
+            plan["middle_at"] + plan["middle_span"] * (step - 1),
+            HEAD_GROUPS + PERIOD * PERIOD_GROUPS * (step - 1 - plan["middle"]),
+        ),
+    )
+    place = base + (plan["padded"] - plan["groups"]) * (base // plan["groups"])
+    return base, jnp.minimum(place // plan["chunk"], plan["last"])
+
+
+def unfold_kernel(plan, flat_ref, in_ref, mid_ref, out_ref, wide_ref, turn_ref):
+    step_at = pl.program_id(0)
+    chunk, margin = plan["chunk"], plan["margin"]
+    base, window = window_of(step_at, plan)
+    shift_by = plan["padded"] - plan["groups"]
 
     def widen(step, carry):
-        at = pl.multiple_of(step * LANES, LANES)
-        wide_ref[pl.ds(at, LANES), :] = flat_ref[pl.ds(at, LANES), :].astype(jnp.float32)
+        place = (window + step) * chunk
+        at = place - shift_by * (place // plan["padded"]) - base + margin
+        source = pl.multiple_of(step * chunk, PERIOD)
+        wide_ref[pl.ds(at, chunk), :] = flat_ref[pl.ds(source, chunk), :].astype(jnp.float32)
         return carry
 
-    lax.fori_loop(0, steps, widen, 0)
-    tail = groups - steps * LANES
-    if tail:
-        wide_ref[pl.ds(steps * LANES, tail), :] = flat_ref[pl.ds(steps * LANES, tail), :].astype(jnp.float32)
+    lax.fori_loop(0, plan["window"] // chunk, widen, 0)
     lane = lax.broadcasted_iota(jnp.int32, (TURN_TILES, LANES), 1)
 
+    def straight(ref):
+        tiles = UNITS // LANES
+
+        def rows16(step, carry):
+            rows = pl.ds(pl.multiple_of(step * PERIOD, PERIOD), PERIOD)
+            for tile in range(tiles):
+                at = margin + step * (PERIOD * tiles) + tile
+                piece = wide_ref[pl.ds(at, PERIOD, stride=tiles), :]
+                ref[rows, pl.ds(tile * LANES, LANES)] = piece.astype(jnp.bfloat16)
+            return carry
+
+        lax.fori_loop(0, ref.shape[0] // PERIOD, rows16, 0)
+
     def period(step, carry):
-        base = step * PERIOD_GROUPS
+        start = margin + step * PERIOD_GROUPS
         for i in range(PERIOD):
             group, shift = divmod(SENONES * i, LANES)
-            value = wide_ref[pl.ds(base + group, TURN_TILES), :]
+            value = wide_ref[pl.ds(start + group, TURN_TILES), :]
             if shift:
-                following = wide_ref[pl.ds(base + group + 1, TURN_TILES), :]
+                following = wide_ref[pl.ds(start + group + 1, TURN_TILES), :]
                 value = pltpu.roll(jnp.where(lane >= shift, value, following), LANES - shift, 1)
             turn_ref[pl.ds(i, TURN_TILES, stride=PERIOD), :] = value
         rows = pl.ds(pl.multiple_of(step * PERIOD, PERIOD), PERIOD)
@@ -78,42 +106,94 @@
             out_ref[rows, pl.ds(tile * LANES, width)] = piece[:, :width]
         return carry
 
-    lax.fori_loop(0, out_ref.shape[0] // PERIOD, period, 0)
-
-
-def unfold(flat):
+    @pl.when(step_at == 0)
+    def _():
+        straight(in_ref)
+
+    @pl.when((step_at > 0) & (step_at <= plan["middle"]))
+    def _():
+        straight(mid_ref)
+
+    @pl.when(step_at > plan["middle"])
+    def _():
+        lax.fori_loop(0, out_ref.shape[0] // PERIOD, period, 0)
+
+
+def unfold(flat, groups, padded):
+    total = flat.shape[0]
     span = PERIOD * PERIOD
-    groups = PERIOD * PERIOD_GROUPS
+    needed = PERIOD * PERIOD_GROUPS
+    middle = 2
+    in_rows = -(-(D_IN + 1) // PERIOD) * PERIOD
+    units = padded // PERIOD
+    chunk = PERIOD * max(f for f in range(1, 51) if units % f == 0)
+    crossed = -(-needed // groups) + 1
+    window = chunk * (-(-(needed + crossed * (padded - groups) + TURN_TILES) // chunk) + 1)
+    plan = dict(
+        groups=groups,
+        padded=padded,
+        chunk=chunk,
+        window=window,
+        last=(total - window) // chunk,
+        margin=window - needed + 2 * chunk,
+        middle=middle,
+        middle_at=(D_IN + 1) * UNITS // LANES,
+        middle_span=UNITS // middle * UNITS // LANES,
+    )
+
+    def middle_map(s):
+        return (jnp.clip(s - 1, 0, middle - 1), 0)
+
     return pl.pallas_call(
-        unfold_kernel,
-        grid=(UNITS // span,),
-        out_shape=jax.ShapeDtypeStruct((UNITS, SENONES), jnp.bfloat16),
+        functools.partial(unfold_kernel, plan),
+        grid=(1 + middle + UNITS // span,),
+        out_shape=(
+            jax.ShapeDtypeStruct((in_rows, UNITS), jnp.bfloat16),
+            jax.ShapeDtypeStruct((UNITS, UNITS), jnp.bfloat16),
+            jax.ShapeDtypeStruct((UNITS, SENONES), jnp.bfloat16),
+        ),
         in_specs=[
-            pl.BlockSpec((pl.Element(groups), pl.Element(LANES)), lambda m: (PERIOD * (HEAD_GROUPS // PERIOD + PERIOD_GROUPS * m), 0))
+            pl.BlockSpec(
+                (pl.Element(window), pl.Element(LANES)), lambda s: (chunk * window_of(s, plan)[1], 0)
+            )
         ],
-        out_specs=pl.BlockSpec((span, SENONES), lambda m: (m, 0)),
+        out_specs=(
+            pl.BlockSpec((in_rows, UNITS), lambda s: (0, 0)),
+            pl.BlockSpec((UNITS // middle, UNITS), middle_map),
+            pl.BlockSpec((span, SENONES), lambda s: (jnp.maximum(s - 1 - middle, 0), 0)),
+        ),
         scratch_shapes=[
-            pltpu.VMEM((groups + TURN_TILES + 16, LANES), jnp.float32),
+            pltpu.VMEM((plan["margin"] + window + chunk, LANES), jnp.float32),
             pltpu.VMEM((TURN_TILES * PERIOD, LANES), jnp.float32),
         ],
     )(flat)
 
 
-def unpack(flat):
-    head = flat[:HEAD_GROUPS].reshape(HEAD_ROWS, UNITS)
-    w_in = head[:D_IN]
-    b_in = head[D_IN]
-    w_mid = head[D_IN + 1 : D_IN + 1 + UNITS]
-    b_mid = head[D_IN + 1 + UNITS]
-    at = HEAD_GROUPS + UNITS * SENONES // LANES
-    b_out = flat[at : at + TILES].reshape(-1)[:SENONES]
-    return (w_in, b_in, w_mid, b_mid, unfold(flat), b_out)
-
-
-def gather_flat(block):
-    rows = block.shape[0] * block.shape[1] // LANES
-    low = block.astype(jnp.bfloat16).reshape(rows, LANES)
-    return lax.all_gather(low, ("node", "wide"), axis=0, tiled=True)
+def flat_slice(flat, groups, padded, begin, count):
+    pieces = []
+    while count:
+        shard, inside = divmod(begin, groups)
+        taken = min(count, groups - inside)
+        pieces.append(flat[shard * padded + inside : shard * padded + inside + taken].reshape(-1))
+        begin, count = begin + taken, count - taken
+    return jnp.concatenate(pieces) if len(pieces) > 1 else pieces[0]
+
+
+def low_flat(block):
+    groups = block.shape[0] * block.shape[1] // LANES
+    low = block.astype(jnp.bfloat16).reshape(groups, LANES)
+    return jnp.pad(low, ((0, -groups % PERIOD), (0, 0)))
+
+
+def gather_params(low, groups):
+    padded = low.shape[0]
+    flat = lax.all_gather(low, ("node", "wide"), axis=0, tiled=True)
+    w_in, w_mid, w_out = unfold(flat, groups, padded)
+    per_row = UNITS // LANES
+    b_in = flat_slice(flat, groups, padded, D_IN * per_row, per_row)
+    b_mid = flat_slice(flat, groups, padded, HEAD_GROUPS - per_row, per_row)
+    b_out = flat_slice(flat, groups, padded, HEAD_GROUPS + UNITS * SENONES // LANES, TILES)[:SENONES]
+    return (w_in[:D_IN], b_in, w_mid, b_mid, w_out, b_out), flat
 
 
 def layer_forward(inputs, weight, bias):
@@ -349,17 +429,22 @@
     node_count = lax.axis_size("node")
     node_at = lax.axis_index("node")
     wide_at = lax.axis_index("wide")
-    params = unpack(gather_flat(master))
+    groups = shard_rows * width // LANES
+    low = low_flat(master)
+    params, flat = gather_params(low, groups)
     w_in, b_in, w_mid, b_mid, w_out, b_out = params
-    words = pack_signs(residual)
-    all_words = lax.all_gather(words, "wide", axis=0, tiled=True).reshape(
-        wide_count, quarter_rows, width // 32
-    )
-    own_words = lax.dynamic_slice_in_dim(all_words, wide_at * shard_rows, shard_rows, 1)
+    low, rest, feats, frame_mask, val_mask = lax.optimization_barrier((low, residual, feats, frame_mask, val_mask))
     stacked = lax.all_gather(stack_frames(feats, utt_lengths[0]), "node", axis=0, tiled=True)
     marks = lax.all_gather(jnp.stack([targets, frame_mask]), "node", axis=1, tiled=True)
     labels = marks[0]
     weights = marks[1].astype(jnp.float32)
+    val_weights = val_mask.astype(jnp.float32)
+    count, val_count = lax.psum((jnp.sum(frame_mask.astype(jnp.float32)), jnp.sum(val_weights)), ("node", "wide"))
+    words, flat = lax.optimization_barrier((pack_signs(rest), flat))
+    all_words = lax.all_gather(words, "wide", axis=0, tiled=True).reshape(
+        wide_count, quarter_rows, width // 32
+    )
+    own_words = lax.dynamic_slice_in_dim(all_words, wide_at * shard_rows, shard_rows, 1)
     sig_one, h_one, sig_two, h_two, logits = run_layers(params, stacked)
     loss_part, lse, hit = frame_terms(logits, labels, weights)
     probs = jnp.exp(logits - lse[:, None])
@@ -401,7 +486,6 @@
         return code((g_out,), offset[None], residual, shard_rows, margin)
 
     residual_new, scales = lax.cond(node_at == 0, first_quarter, other_quarter, 0)
-    loss_sum, count = lax.psum((loss_part, jnp.sum(weights)), "wide")
     all_scales = lax.all_gather(scales, "wide", axis=0, tiled=True).reshape(
         wide_count, wide_count, width
     )
@@ -420,12 +504,12 @@
         first_hat / (jnp.sqrt(second_hat) + EPS_ADAM) + DECAY * master
     )
     average_new = AVG_KEEP * average + (1.0 - AVG_KEEP) * master_new
-    val_params = unpack(gather_flat(average_new))
+    val_params, _ = gather_params(low_flat(average_new), groups)
     val_stacked = stack_frames(val_feats, jnp.full((1,), val_feats.shape[0], jnp.int32))
     val_logits = run_layers(val_params, val_stacked)[4]
-    val_weights = val_mask.astype(jnp.float32)
     val_part = frame_terms(val_logits, val_targets, val_weights)[0]
-    val_sum, val_count = lax.psum((val_part, jnp.sum(val_weights)), ("node", "wide"))
+    loss_own = jnp.where(node_at == 0, loss_part, 0.0)
+    loss_sum, val_sum = lax.psum((loss_own, val_part), ("node", "wide"))
     return (
         loss_sum / count,
         val_sum / val_count,

time: 1380 us -> 1200 us (0.87)
  local copies, waits for them, and re-layouts: 206 us -> 89.6 us
  waiting for transfers between devices: 530 us -> 437 us
  Pallas kernels: 204 us -> 228 us
    unnamed x55 -> x45, local copies, waits for them, and re-layouts: 136 us -> 28.3 us
    all_gather x2, waiting for transfers between devices: 509 us -> 437 us  [gather_params(): flat = lax.all_gather(low, ('node', 'wide'), axis=0, tiled=True)]
    slice x10 -> x0, local copies, waits for them, and re-layouts: 45.1 us -> none  [the longest x4 41.2 us: unpack(): w_mid = head[D_IN + 1:D_IN + 1 + UNITS]]
    optimization_barrier x0 -> x2, local copies, waits for them, and re-layouts: none -> 24.7 us  [body(): lax.optimization_barrier((low, residual, feats, frame_mask, val_mask))]
    pallas_call x2, Pallas kernels: 128 us -> 153 us  [unfold(): pl.pallas_call(functools.partial(unfold_kernel, plan), grid=(1 + middle +...]
    all_gather x1, waiting for transfers between devices: 20.6 us -> 0.02 us  [body(): lax.all_gather(words, 'wide', axis=0, tiled=True)]
    psum x3 -> x2, blocking collectives: 91.5 us -> 76.3 us  [the longest x1 38.6 us: body(): loss_sum, val_sum = lax.psum((loss_own, val_part), ('node', 'wide'))]
  transfers between devices with their start and end apart: 3 -> 3, of which waited for: 3 -> 2; matrix products, arithmetic and copies ran while one was open for 3% -> 25% of each run, Pallas kernels for 0% -> 13%
where the time goes in v2:
time: 1200 us; the launch traced here: 1180 us
  waiting for transfers between devices  437 us (36%)
  Pallas kernels  228 us (19%)
  matrix products  196 us (16%)
  blocking collectives  122 us (10%)
  local copies, waits for them, and re-layouts  89.6 us (7%)
  other arithmetic  81.8 us (7%)
  between operations  23.1 us (2%)
    all_gather x2, waiting for transfers between devices, gather_params(): flat = lax.all_gather(low, ('node', 'wide'), axis=0, tiled=True)  437 us
    pallas_call x2, Pallas kernels, unfold(): pl.pallas_call(functools.partial(unfold_kernel, plan), grid=(1 + middle +...  153 us
    dot_general x5, matrix products, layer_forward(): jnp.dot(inputs, weight, preferred_element_type=jnp.float32)  97.1 us
    pallas_call x1, Pallas kernels, code(): pl.pallas_call(functools.partial(code_kernel, plan), out_shape=(jax.Shape...  75.1 us
    dot_general x1, matrix products, contract_columns(): lax.dot_general(left, right, (((1,), (1,)), ((), ())), preferred_element_...  51.2 us
    dot_general x3, matrix products, contract_rows(): lax.dot_general(left, right, (((0,), (0,)), ((), ())), preferred_element_...  47.6 us
    psum x1, blocking collectives, body(): loss_sum, val_sum = lax.psum((loss_own, val_part), ('node', 'wide'))  38.6 us
    psum x1, blocking collectives, body(): lax.psum((jnp.sum(frame_mask.astype(jnp.float32)), jnp.sum(val_weights)),...  37.7 us
  transfers between devices with their start and end apart: 3, of which 2 were waited for; matrix products, arithmetic and copies ran while one was open for 25% of the time, Pallas kernels for 13%

profile of v2, /device:TPU:0, one launch (start us, length us, event | category | flops | bytes accessed | tf_op | source)
XLA Modules:
  0.0 1178.2 jit_solution(16821474075791801213)
XLA Ops:
  7.2 3.3 convert_element_type.101
  10.5 3.6 reshape.311
  14.2 2.6 pad.7
  16.9 2.4 copy.70
  19.3 0.2 reduce-window.6
  19.6 0.1 compare_select_fusion
  19.7 0.2 reshape.331
  20.1 5.6 gather_fusion
  25.7 0.4 reshape.314
  26.1 4.1 copy.64
  30.2 0.2 copy-done.5
  30.4 2.4 copy.68
  32.8 24.5 %copy.65 = f32[11800,512]{0,1:T(8,128)} copy(f32[11800,512]{1,0:T(8,128)} %param.26) | data formatting | bytes 48332800 | tf_op jit(solution)/shard_map/optimization_barrier | solution.py:436
  57.3 9.6 all_gather.18
  66.9 0.6 convert_reduce_fusion
  67.5 22.2 %all_gather.19 = bf16[1024,440]{1,0:T(8,128)(2,1)S(1)} all-gather(bf16[256,440]{1,0:T(8,128)(2,1)S(1)} %reshape.314), channel_id=1, replica_groups=mesh['node'=4,'wide'=8] {'node'}, dimensions={0}, use_global_device_ids=true | all-gather | bytes 1126400 | tf_op jit(solution)/shard_map/all_gather | solution.py:437
  89.7 0.6 fusion.45
  90.3 11.6 shift-left_reduce_fusion
  101.9 190.2 %all-gather.5.cloned.1.call-done.flat_ref = bf16[188928,128]{1,0:T(8,128)(2,1)} async-done(((bf16[5904,128]{1,0:T(8,128)(2,1)}), bf16[188928,128]{1,0:T(8,128)(2,1)}) %all-gather.5.cloned.1.call-update) | async-done | bytes 48365584 | tf_op jit(solution)/shard_map/all_gather | solution.py:190
  292.1 0.7 slice_bitcast_fusion.1
  292.9 0.7 fusion.39
  293.6 76.3 %shard_map.201 = (bf16[448,2048]{1,0:T(8,128)(2,1)}, bf16[2048,2048]{1,0:T(8,128)(2,1)}, bf16[2048,9304]{1,0:T(8,128)(2,1)}) custom-call(bf16[188928,128]{1,0:T(8,128)(2,1)} %all-gather.5.cloned.1.call-done.flat_ref), custom_call_target="tpu_custom_call" | custom-call | tf_op jit(solution)/shard_map/pallas_call | solution.py:147
  369.9 7.0 fusion.46
  377.0 11.9 %fusion.47 = (bf16[1024,2048]{1,0:T(8,128)(2,1)S(1)}, f32[1024,2048]{1,0:T(8,128)}) fusion(f32[2048]{0:T(1024)S(1)} %get-tuple-element.190, bf16[1024,2048]{1,0:T(8,128)(2,1)S(1)} %get-tuple-element.193, bf16[2048,2048]{1,0:T(8,128)(2,1)S(1)} %copy-done.16), kind=kOutput, calls=%fused_computation.101 | convolution fusion | flops 8600420352 | bytes 25174016 | tf_op jit(solution)/shard_map/dot_general | solution.py:200
  388.8 51.4 %add_reduce_fusion = (f32[1024]{0:T(1024)S(1)}, f32[1024,9304]{0,1:T(8,128)}) fusion(f32[9304]{0:T(1024)S(1)} %slice_convert_fusion.1, bf16[1024,2048]{1,0:T(8,128)(2,1)S(1)} %get-tuple-element.195, bf16[2048,9304]{1,0:T(8,128)(2,1)} %get-tuple-element.70), kind=kOutput, calls=%fused_computation.28 | convolution fusion | flops 39042859008 | bytes 80453984 | tf_op jit(solution)/shard_map/dot_general | solution.py:200
  440.2 17.7 %select_reduce_fusion = (f32[1024]{0:T(1024)S(1)}, f32[1024]{0:T(1024)S(1)}) fusion(f32[1024,9304]{0,1:T(8,128)} %get-tuple-element.198, s32[1024]{0:T(1024)S(1)} %bitcast.69, f32[9304]{0:T(1024)S(1)} %slice_convert_fusion.1, f32[1024]{0:T(1024)S(1)} %get-tuple-element.197), kind=kLoop, calls=%fused_computation.25 | loop fusion | flops 57161728 | bytes 38162784 | tf_op jit(solution)/shard_map/reduce_sum | solution.py:225
  457.9 0.6 multiply_reduce_fusion.2
  458.5 25.2 %fusion.19 = bf16[1024,9304]{0,1:T(8,128)(2,1)} fusion(f32[1024,9304]{0,1:T(8,128)} %get-tuple-element.198, f32[1024]{0:T(1024)S(1)} %get-tuple-element.186, f32[1024]{0:T(1024)S(1)} %bitcast.72, s32[1024]{0:T(1024)S(1)} %bitcast.70, f32[9304]{0:T(1024)S(1)} %slice_convert_fusion.1), kind=kLoop, calls=%fused_computation.24 | loop fusion | flops 66691072 | bytes 57213280 | tf_op jit(solution)/shard_map/convert_element_type | solution.py:451
  483.8 182.4 %conditional.1 = ((f32[11800,512]{1,0:T(8,128)}, f32[8,512]{1,0:T(8,128)S(1)})) conditional(s32[]{:T(128)} %convert_element_type.114, (s32[]{:T(128)}, bf16[1024,2048]{1,0:T(8,128)(2,1)}, bf16[1024,9304]{0,1:T(8,128)(2,1)}, f32[11800,512]{1,0:T(8,128)}) %tuple.62, (bf16[1024,440]{1,0:T(8,128)(2,1)S(1)}, bf16[1024,9304]{0,1:T(8,128)(2,1)}, ...), branch_computations={%region_11.12_spmd.clone, %region_12.13_spmd} | conditional | flops 60673015808 | bytes 153447264 | solution.py:488
  484.1 7.7 concatenate.8
  491.8 14.5 %fusion.11.refs_2_ = f32[112,9304]{1,0:T(8,128)} fusion(bf16[1024,9304]{0,1:T(8,128)(2,1)} %get-tuple-element.151, bf16[1024,2048]{1,0:T(8,128)(2,1)} %get-tuple-element.43), kind=kOutput, calls=%fused_computation.15 | convolution fusion | flops 2134114304 | bytes 23484928 | tf_op jit(solution)/shard_map/cond/branch_1_fun/dot_general | solution.py:204
  506.3 51.2 %fusion.1 = bf16[1024,2048]{1,0:T(8,128)(2,1)} fusion(f32[1024,2048]{1,0:T(8,128)} %get-tuple-element.39, bf16[1024,9304]{0,1:T(8,128)(2,1)} %get-tuple-element.151, bf16[2048,9304]{1,0:T(8,128)(2,1)} %get-tuple-element.38), kind=kOutput, calls=%fused_computation.5 | convolution fusion | flops 39032193024 | bytes 69746688 | tf_op jit(solution)/shard_map/cond/branch_1_fun/dot_general | solution.py:208
  557.5 17.6 %fusion.4.refs_0_ = f32[520,2048]{1,0:T(8,128)} fusion(f32[1024,2048]{1,0:T(8,128)} %get-tuple-element.41, bf16[1024,2048]{1,0:T(8,128)(2,1)} %fusion.1, bf16[2048,2048]{1,0:T(8,128)(2,1)} %get-tuple-element.40, bf16[1024,1]{1,0:T(8,128)(2,1)S(1)} %broadcast.253, bf16[1024,440]{1,0:T(8,128)(2,1)S(1)} %get-tuple-element.36, bf16[520]{0:T(1024)(128)(2,1)S(1)} %pad.11.clone), kind=kOutput, calls=%fused_computation.8 | convolution fusion | flops 10782556160 | bytes 26135568 | tf_op jit(solution)/shard_map/cond/branch_1_fun/dot_general | solution.py:204
  575.1 15.5 %fusion.49.refs_1_ = f32[2080,2048]{1,0:T(8,128)} fusion(bf16[1024,2080]{1,0:T(8,128)(2,1)} %concatenate.8, bf16[1024,2048]{1,0:T(8,128)(2,1)} %fusion.1), kind=kOutput, calls=%fused_computation.103 | convolution fusion | flops 8724152320 | bytes 25493504 | tf_op jit(solution)/shard_map/cond/branch_1_fun/dot_general | solution.py:204
  590.6 75.1 %branch_1_fun.1 = (f32[11800,512]{1,0:T(8,128)}, f32[8,512]{1,0:T(8,128)S(1)}) custom-call(s32[1]{0:T(128)} %constant.36.clone.offset_ref, f32[520,2048]{1,0:T(8,128)} %fusion.4.refs_0_, f32[2080,2048]{1,0:T(8,128)} %fusion.49.refs_1_, f32[112,9304]{1,0:T(8,128)} %fusion.11.refs_2_, f32[11800,512]{1,0:T(8,128)} %get-tuple-element.44.refs_3_), custom_call_target="tpu_custom_call" | custom-call | tf_op jit(solution)/shard_map/cond/branch_1_fun/pallas_call | solution.py:388
  666.2 14.0 %all_gather.22 = f32[64,512]{1,0:T(8,128)S(1)} all-gather(f32[8,512]{1,0:T(8,128)S(1)} %get-tuple-element.74), channel_id=1, replica_groups=mesh['node'=4,'wide'=8] {'wide'}, dimensions={0}, use_global_device_ids=true | all-gather | bytes 147456 | tf_op jit(solution)/shard_map/all_gather | solution.py:489
  680.3 1.4 constant_dynamic-slice_fusion
  681.7 6.3 multiply_reduce_fusion
  688.0 1.4 multiply_reduce_fusion.1
  689.4 3.5 copy.63
  692.9 37.7 %all-reduce.3 = (f32[]{:T(128)}, f32[]{:T(128)}) all-reduce(f32[]{:T(128)} %convert_reduce_fusion, f32[]{:T(128)} %multiply_reduce_fusion.1), channel_id=1, replica_groups=mesh['node'=4,'wide'=8] {'node','wide'}, use_global_device_ids=true, to_apply=%region_9.10 | all-reduce | flops 2 | bytes 16 | tf_op jit(solution)/shard_map/psum | solution.py:442
  732.8 0.4 broadcast_multiply_fusion
  733.2 1.5 copy-done
  734.7 1.0 copy-done.1
  735.6 8.5 fusion.43
  744.2 2.6 copy.71
  746.7 3.6 reshape.321
  750.4 2.6 pad.8
  753.3 0.2 reshape.339
  753.5 3.3 gather_fusion.1
  756.8 0.9 reshape.316
  758.4 3.5 copy.75
  761.9 3.8 copy.72
  765.7 3.5 copy.73
  769.2 2.3 copy.74
  771.5 247.1 %all-gather.7.cloned.1.call-done.flat_ref = bf16[188928,128]{1,0:T(8,128)(2,1)} async-done(((bf16[5904,128]{1,0:T(8,128)(2,1)}), bf16[188928,128]{1,0:T(8,128)(2,1)}) %all-gather.7.cloned.1.call-update) | async-done | bytes 48365584 | tf_op jit(solution)/shard_map/all_gather | solution.py:190
  1018.5 0.7 slice_bitcast_fusion
  1019.3 0.7 fusion.36
  1020.0 76.4 %shard_map.202 = (bf16[448,2048]{1,0:T(8,128)(2,1)}, bf16[2048,2048]{1,0:T(8,128)(2,1)}, bf16[2048,9304]{1,0:T(8,128)(2,1)}) custom-call(bf16[188928,128]{1,0:T(8,128)(2,1)} %all-gather.7.cloned.1.call-done.flat_ref), custom_call_target="tpu_custom_call" | custom-call | tf_op jit(solution)/shard_map/pallas_call | solution.py:147
  1096.4 2.1 fusion.29
  1098.5 24.7 %fusion.48 = (f32[128]{0:T(128)S(1)}, f32[128,9304]{0,1:T(8,128)}) fusion(f32[9304]{0:T(1024)S(1)} %slice_convert_fusion, bf16[2048,9304]{1,0:T(8,128)(2,1)} %get-tuple-element.77, bf16[128,2048]{1,0:T(8,128)(2,1)S(1)} %fusion.29, bf16[2048,2048]{1,0:T(8,128)(2,1)} %get-tuple-element.76, f32[2048]{0:T(1024)S(1)} %get-tuple-element.187), kind=kOutput, calls=%fused_computation.102 | convolution fusion | flops 5955409920 | bytes 51831648 | tf_op jit(solution)/shard_map/dot_general | solution.py:200
  1123.2 3.0 exponential_reduce_fusion.1
  1126.2 0.6 convert_reduce_fusion.1
  1126.9 38.6 %all-reduce.2 = (f32[]{:T(128)}, f32[]{:T(128)}, f32[]{:T(128)}) all-reduce(f32[]{:T(128)S(6)} %select_n.76, f32[]{:T(128)} %get-tuple-element.174, f32[]{:T(128)} %get-tuple-element.173), channel_id=1, replica_groups=mesh['node'=4,'wide'=8] {'node','wide'}, use_global_device_ids=true, to_apply=%region_7.8 | all-reduce | flops 3 | bytes 24 | tf_op jit(solution)/shard_map/psum | solution.py:512
  (59 shorter events, 1.0 us)
Async XLA Ops:
  7.2 9.7 copy-start.2
  7.2 284.9 %all-gather.5.cloned.1.call-start = ((), (), s32[]{:S(2)}) async-start(), calls=%async_computation | async-start | bytes 49876992 | tf_op jit(solution)/shard_map/all_gather | solution.py:190
  14.2 5.1 copy-start.17
  14.2 5.8 copy-start.8
  16.8 663.4 %all-gather.9.cloned.1.call-start = ((), (), s32[]{:S(2)}) async-start(), calls=%async_computation.2 | async-start | bytes 6856704 | tf_op jit(solution)/shard_map/all_gather | solution.py:444
  19.5 0.6 copy-start.10
  26.1 4.3 copy-start.5
  32.8 24.6 %copy-start.12 = (s32[256]{0:T(256)S(1)}, s32[256]{0:T(256)}, u32[]{:S(2)}) copy-start(s32[256]{0:T(256)} %param.19) | copy-start | bytes 3076
  32.8 24.6 %copy-start.13 = (s32[256]{0:T(256)S(1)}, s32[256]{0:T(256)}, u32[]{:S(2)}) copy-start(s32[256]{0:T(256)} %param.18) | copy-start | bytes 3076
  292.9 725.7 %all-gather.7.cloned.1.call-start = ((), (), s32[]{:S(2)}) async-start(), calls=%async_computation.1 | async-start | bytes 49876992 | tf_op jit(solution)/shard_map/all_gather | solution.py:190
  369.9 7.0 copy-start.16
  376.9 11.9 %copy-start.4 = (bf16[1024,2048]{1,0:T(8,128)(2,1)}, bf16[1024,2048]{1,0:T(8,128)(2,1)S(1)}, u32[]{:S(2)}) copy-start(bf16[1024,2048]{1,0:T(8,128)(2,1)S(1)} %get-tuple-element.193) | copy-start | bytes 12582916
  388.8 51.4 %copy-start.3 = (bf16[1024,2048]{1,0:T(8,128)(2,1)}, bf16[1024,2048]{1,0:T(8,128)(2,1)S(1)}, u32[]{:S(2)}) copy-start(bf16[1024,2048]{1,0:T(8,128)(2,1)S(1)} %get-tuple-element.195) | copy-start | bytes 12582916
  440.2 17.7 %copy-start.7 = (f32[1,1024]{1,0:T(1,128)S(1)}, f32[1,1024]{1,0:T(1,128)}, u32[]{:S(2)}) copy-start(f32[1,1024]{1,0:T(1,128)} %get-tuple-element.192) | copy-start | bytes 12292
  732.8 1.9 copy-start
  732.8 2.8 copy-start.1
  744.2 8.9 copy-start.9
  744.2 9.0 copy-start.11
  1020.0 76.4 %copy-start.6 = (bf16[128,440]{1,0:T(8,128)(2,1)S(1)}, bf16[128,440]{1,0:T(8,128)(2,1)}, u32[]{:S(2)}) copy-start(bf16[128,440]{1,0:T(8,128)(2,1)} %reshape.316) | copy-start | bytes 337924
  1098.5 24.8 %copy-start.14 = (s32[128]{0:T(128)S(1)}, s32[128]{0:T(128)}, u32[]{:S(2)}) copy-start(s32[128]{0:T(128)} %param.22) | copy-start | bytes 1540
  1098.5 27.8 %copy-start.15 = (s32[128]{0:T(128)S(1)}, s32[128]{0:T(128)}, u32[]{:S(2)}) copy-start(s32[128]{0:T(128)} %param.21) | copy-start | bytes 1540
Sparse Core Ops, SparseCore 0:
  17.0 275.0 all-gather.4
  294.3 61.2 all-gather.8
  753.1 265.3 all-gather.6
